TPU v7x, 256 devices: a whole 4x4x8 slice. The times are simulated.
256 devices in a mesh: ctx: 32 (over z, x_hi, core), head: 8 (over y, x_lo).
Axes of the slice: x: 4 (x_hi: 2, x_lo: 2; x = x_hi * 2 + x_lo), y: 4, z: 8, core: 2. Of those that a mesh axis runs over, the one named last changes fastest.
Arguments:
- queries: bfloat16 [8192, 8192], P('ctx', 'head'), may hold values from -10 to 10
- key_rows: bfloat16 [8192, 1024], P('ctx', 'head'), may hold values from -4.5 to 4.5
- values: bfloat16 [8192, 1024], P('ctx', 'head'), may hold values from -24 to 24
- lengths: int32 [17], replicated, may hold values from 1 to 4352, as said below
- block_plan: int32 [1024], P('ctx'), may hold values from 0 to 1023, as said below
- inverse: int32 [1024], replicated, may hold values from 0 to 1023, as said below
- mask_lo: int32 [1024], replicated, may hold values from 0 to 1023, as said below
- out_weight: bfloat16 [8192, 4096], P('head'), may hold values from -0.375 to 0.375
Outputs:
- mixed_out: bfloat16 [8192, 4096], P('ctx', 'head')
Inputs may be any that keep to these rules, and one draw needn't show every extreme that they name: One document has exactly 4352 tokens, every other is shorter; the lengths sum to 8192. A permutation of the 1024 blocks; slot block_plan[b] lies on index block_plan[b] // 32 of ctx; every index receives exactly 32 blocks, and at most 2 blocks of one index go to any one index, which is reached in every draw. inverse[block_plan[b]] == b. mask_lo[b] lies between the block holding the first token of the document of block b's first token and b, both included.
All inputs are finite; a program needn't handle non-finite values.
Results may differ from a plain program's by a relative error of at most 0.02.
Values may be sent and summed in bfloat16 or wider, within the bound.
A program may use at most 64 MiB of HBM per device.

v0:
```python
import jax
import jax.numpy as jnp
from jax import lax
from jax.sharding import PartitionSpec as P

HD = 128
BLK = 8
NEG_FILL = -1e30


def document_of(positions, doc_ends):
    return jnp.sum((positions[:, None] >= doc_ends[None, :]).astype(jnp.int32), axis=1)


def rank_within(owners, order_keys):
    same_owner = owners[:, None] == owners[None, :]
    comes_first = order_keys[None, :] < order_keys[:, None]
    return jnp.sum((same_owner & comes_first).astype(jnp.int32), axis=1)


def slot_sources(owners, order_ranks, device_count, capacity):
    device_ids = jnp.arange(device_count, dtype=jnp.int32)
    slot_ids = jnp.arange(capacity, dtype=jnp.int32)
    entry_ids = jnp.arange(owners.shape[0], dtype=jnp.int32)
    matches = (owners[None, None, :] == device_ids[:, None, None]) & (
        order_ranks[None, None, :] == slot_ids[None, :, None]
    )
    sources = jnp.sum(jnp.where(matches, entry_ids[None, None, :], 0), axis=2)
    return (sources.reshape(-1), jnp.any(matches, axis=2).reshape(-1))


def pack_blocks(block_data, sources, occupied, device_count, capacity):
    picked = jnp.take(block_data, sources, axis=0)
    picked = jnp.where(occupied[:, None, None], picked, jnp.zeros((), block_data.dtype))
    return picked.reshape((device_count, capacity) + block_data.shape[1:])


def unpack_blocks(received, owners, order_ranks, capacity):
    merged = received.reshape((-1,) + received.shape[2:])
    picked = jnp.take(merged, owners * capacity + order_ranks, axis=0)
    return picked.reshape((-1, picked.shape[-1]))


def project(attended, out_weight):
    partial_value = jnp.dot(attended, out_weight, preferred_element_type=jnp.float32).astype(
        jnp.bfloat16
    )
    summed = lax.psum_scatter(partial_value, "head", scatter_dimension=1, tiled=True).astype(
        jnp.float32
    )
    return summed.astype(jnp.bfloat16)


def attend_all(held_queries, held_pairs, root, doc_ends, mask_lo, key_position):
    row_count, query_width = held_queries.shape
    kv_width = held_pairs.shape[1] // 2
    kv_heads = kv_width // HD
    group_size = query_width // (kv_heads * HD)
    score_scale = HD ** (-0.5)
    offsets = jnp.arange(BLK, dtype=jnp.int32)
    query_pos = (root[:, None] * BLK + offsets[None, :]).reshape(row_count)
    query_doc = document_of(query_pos, doc_ends)
    table_ids = jnp.arange(mask_lo.shape[0], dtype=jnp.int32)
    block_lo = jnp.sum(jnp.where(root[:, None] == table_ids[None, :], mask_lo[None, :], 0), axis=1)
    query_lo = jnp.repeat(block_lo, BLK)
    query_heads = held_queries.reshape(row_count, kv_heads, group_size, HD)

    def one_step(state_now, kv_piece, first_key):
        key_width = kv_piece.shape[0]
        key_ids = first_key + jnp.arange(key_width, dtype=jnp.int32)
        key_pos = key_position(key_ids)
        key_doc = document_of(key_pos, doc_ends)
        allowed = (
            (query_doc[:, None] == key_doc[None, :])
            & (key_pos[None, :] <= query_pos[:, None])
            & ((key_pos // BLK)[None, :] >= query_lo[:, None])
        )
        run_max, run_sum, run_acc = state_now
        key_heads = kv_piece[:, :kv_width].reshape(key_width, kv_heads, HD)
        value_heads = kv_piece[:, kv_width:].reshape(key_width, kv_heads, HD)
        scores = (
            jnp.einsum("tkgd,skd->tkgs", query_heads, key_heads, preferred_element_type=jnp.float32)
            * score_scale
        )
        mask_full = allowed[:, None, None, :]
        scores = jnp.where(mask_full, scores, NEG_FILL)
        new_max = jnp.maximum(run_max, jnp.max(scores, axis=-1))
        weights = jnp.where(mask_full, jnp.exp(scores - new_max[..., None]), 0.0)
        fading = jnp.exp(run_max - new_max)
        new_sum = run_sum * fading + jnp.sum(weights, axis=-1)
        update = jnp.einsum(
            "tkgs,skd->tkgd",
            weights.astype(jnp.bfloat16),
            value_heads,
            preferred_element_type=jnp.float32,
        )
        return (new_max, new_sum, run_acc * fading[..., None] + update)

    stat_shape = (row_count, kv_heads, group_size)
    initial = (
        jnp.full(stat_shape, NEG_FILL, jnp.float32),
        jnp.zeros(stat_shape, jnp.float32),
        jnp.zeros(stat_shape + (HD,), jnp.float32),
    )
    kv_piece = lax.all_gather(held_pairs, "ctx", axis=0, tiled=True)
    piece_rows = kv_piece.shape[0]
    key_width = 256

    def loop_body(step_index, state_in):
        offset_rows = step_index * key_width
        sub_piece = lax.dynamic_slice_in_dim(kv_piece, offset_rows, key_width, 0)
        return one_step(state_in, sub_piece, offset_rows)

    run_max, run_sum, run_acc = lax.fori_loop(0, piece_rows // key_width, loop_body, initial)
    return (run_acc / run_sum[..., None]).astype(jnp.bfloat16).reshape(row_count, query_width)


def on_device(queries, key_rows, values, lengths, block_plan, inverse, mask_lo, out_weight):
    row_count, query_width = queries.shape
    block_count = row_count // BLK
    device_count = lax.axis_size("ctx")
    capacity = max(2, block_count // device_count + 1)
    here_index = lax.axis_index("ctx")
    doc_ends = jnp.cumsum(lengths)
    key_values = jnp.concatenate([key_rows, values], axis=1)
    pair_width = key_values.shape[1]
    local_ids = jnp.arange(block_count, dtype=jnp.int32)
    dest_dev = block_plan // block_count
    dest_slot = block_plan % block_count
    send_rank = rank_within(dest_dev, dest_slot)
    sources, occupied = slot_sources(dest_dev, send_rank, device_count, capacity)
    send_queries = pack_blocks(
        queries.reshape(block_count, BLK, query_width), sources, occupied, device_count, capacity
    )
    send_pairs = pack_blocks(
        key_values.reshape(block_count, BLK, pair_width), sources, occupied, device_count, capacity
    )
    got_queries, got_pairs = (
        lax.all_to_all(send_queries, "ctx", split_axis=0, concat_axis=0, tiled=True),
        lax.all_to_all(send_pairs, "ctx", split_axis=0, concat_axis=0, tiled=True),
    )
    root = lax.dynamic_slice_in_dim(inverse, here_index * block_count, block_count)
    from_dev = root // block_count
    recv_rank = rank_within(from_dev, local_ids)
    held_queries = unpack_blocks(got_queries, from_dev, recv_rank, capacity)
    held_pairs = unpack_blocks(got_pairs, from_dev, recv_rank, capacity)

    def key_position(key_ids):
        return jnp.take(inverse, key_ids // BLK) * BLK + key_ids % BLK

    held_att = attend_all(held_queries, held_pairs, root, doc_ends, mask_lo, key_position)
    back_sources, back_occupied = slot_sources(from_dev, recv_rank, device_count, capacity)
    send_att = pack_blocks(
        held_att.reshape(block_count, BLK, query_width),
        back_sources,
        back_occupied,
        device_count,
        capacity,
    )
    back_att = lax.all_to_all(send_att, "ctx", split_axis=0, concat_axis=0, tiled=True)
    mixed_out = project(unpack_blocks(back_att, dest_dev, send_rank, capacity), out_weight)
    return mixed_out


def solution(mesh):
    in_specs = (
        P("ctx", "head"),
        P("ctx", "head"),
        P("ctx", "head"),
        P(),
        P("ctx"),
        P(),
        P(),
        P("head", None),
    )
    out_specs = P("ctx", "head")
    return jax.shard_map(
        on_device, mesh=mesh, in_specs=in_specs, out_specs=out_specs, check_vma=False
    )
```

profile of v0, /device:TPU:1, one launch (start us, length us, event | category | flops | bytes accessed | tf_op | source)
XLA Modules:
  0.0 449.5 jit_solution(887218490249605697)
XLA Ops:
  10.5 12.6 %all-to-all-start = ((bf16[32,2,8,256]{3,2,1,0:T(8,128)(2,1)}), bf16[32,2,8,256]{3,2,1,0:T(8,128)(2,1)S(1)}, u32[]{:S(2)}, u32[]{:S(2)}) async-start(bf16[32,2,8,256]{3,2,1,0:T(8,128)(2,1)} %select_select_fusion.2), calls=%async_computation | async-start | bytes 524288 | tf_op jit(solution)/shard_map/all_to_all | solution.py:140
  24.3 11.7 %all-to-all-done = bf16[32,2,8,256]{3,2,1,0:T(8,128)(2,1)S(1)} async-done(((bf16[32,2,8,256]{3,2,1,0:T(8,128)(2,1)}), bf16[32,2,8,256]{3,2,1,0:T(8,128)(2,1)S(1)}, u32[]{:S(2)}, u32[]{:S(2)}) %all-to-all-start) | async-done | bytes 262176 | tf_op jit(solution)/shard_map/all_to_all | solution.py:140
  39.6 4.1 all-to-all-start.1
  45.2 31.0 %all-to-all-done.1 = bf16[32,2,8,1024]{3,2,1,0:T(8,128)(2,1)S(1)} async-done(((bf16[32,2,8,1024]{3,2,1,0:T(8,128)(2,1)}), bf16[32,2,8,1024]{3,2,1,0:T(8,128)(2,1)S(1)}, u32[]{:S(2)}, u32[]{:S(2)}) %all-to-all-start.1) | async-done | bytes 1048608 | tf_op jit(solution)/shard_map/all_to_all | solution.py:139
  77.1 48.6 %all-gather.2.cloned.1.call-done = bf16[8192,256]{1,0:T(8,128)(2,1)} async-done(((bf16[256,256]{1,0:T(8,128)(2,1)}), bf16[8192,256]{1,0:T(8,128)(2,1)}) %all-gather.2.cloned.1.call-update) | async-done | bytes 4194320 | tf_op jit(solution)/shard_map/all_gather | solution.py:105
  125.7 220.3 %while.21 = (s32[]{:T(128)}, f32[256,1,8]{0,2,1:T(8,128)S(1)}, f32[256,1,8]{0,2,1:T(8,128)S(1)}, f32[256,1,8,128]{0,3,2,1:T(8,128)}, s32[256]{0:T(256)S(1)}, /*i...) while((s32[]{:T(128)}, f32[256,1,8]{0,2,1:T(8,128)S(1)}, ...), condition=%wide.region_12.15_spmd.clone, body=%wide.region_8.14_spmd.clone.sunk | while | flops 276407808 | bytes 9464371 | solution.py:114
  125.8 1.4 gather_fusion
  129.1 2.5 fusion.44
  132.2 1.4 gather_fusion
  135.6 2.9 fusion.44
  142.5 2.9 fusion.44
  149.4 2.9 fusion.44
  156.3 2.9 fusion.44
  163.2 2.9 fusion.44
  170.1 2.9 fusion.44
  177.0 2.9 fusion.44
  183.9 2.9 fusion.44
  187.4 1.4 gather_fusion
  190.8 2.9 fusion.44
  197.7 2.9 fusion.44
  204.6 2.9 fusion.44
  211.5 2.9 fusion.44
  218.4 2.9 fusion.44
  225.3 2.9 fusion.44
  232.2 2.9 fusion.44
  239.0 2.9 fusion.44
  245.9 2.9 fusion.44
  249.5 1.4 gather_fusion
  252.8 2.9 fusion.44
  256.4 1.4 gather_fusion
  259.7 2.9 fusion.44
  266.6 2.9 fusion.44
  273.5 2.9 fusion.44
  280.4 2.9 fusion.44
  287.3 2.9 fusion.44
  294.2 2.9 fusion.44
  301.1 2.9 fusion.44
  308.0 2.9 fusion.44
  314.9 2.9 fusion.44
  318.5 1.4 gather_fusion
  321.8 2.9 fusion.44
  328.7 2.9 fusion.44
  335.6 2.9 fusion.44
  342.5 2.9 fusion.44
  349.7 4.6 %all-to-all-start.2 = ((bf16[32,2,8,1024]{3,2,1,0:T(8,128)(2,1)}), bf16[32,2,8,1024]{3,2,1,0:T(8,128)(2,1)S(1)}, u32[]{:S(2)}, u32[]{:S(2)}) async-start(bf16[32,2,8,1024]{3,2,1,0:T(8,128)(2,1)} %bitcast.10), calls=%async_computation.2 | async-start | bytes 2097152 | tf_op jit(solution)/shard_map/all_to_all | solution.py:160
  354.4 28.1 %all-to-all-done.2 = bf16[32,2,8,1024]{3,2,1,0:T(8,128)(2,1)S(1)} async-done(((bf16[32,2,8,1024]{3,2,1,0:T(8,128)(2,1)}), bf16[32,2,8,1024]{3,2,1,0:T(8,128)(2,1)S(1)}, u32[]{:S(2)}, u32[]{:S(2)}) %all-to-all-start.2) | async-done | bytes 1048608 | tf_op jit(solution)/shard_map/all_to_all | solution.py:160
  383.1 7.1 %convolution_convert_fusion = bf16[256,4096]{1,0:T(8,128)(2,1)} fusion(bf16[1024,4096]{1,0:T(8,128)(2,1)} %param.21, bf16[32,8,1024]{2,1,0:T(8,128)(2,1)S(1)} %gather_fusion.6, pred[32]{0:T(512)(128)(4,1)S(1)} %get-tuple-element.401), kind=kOutput, calls=%fused_computation.58 | convolution fusion | flops 2148794368 | bytes 11010080 | tf_op jit(solution)/shard_map/dot_general | solution.py:45
  390.2 52.4 %reduce-scatter.2.cloned.1.call-done = bf16[256,512]{1,0:T(8,128)(2,1)} async-done(((bf16[256,4096]{1,0:T(8,128)(2,1)}), bf16[256,512]{1,0:T(8,128)(2,1)}) %reduce-scatter.2.cloned.1.call-update) | async-done | bytes 262160 | tf_op jit(solution)/shard_map/reduce_scatter | solution.py:48
  (551 shorter events, 130.1 us)
Async XLA Ops:
  6.5 31.1 %copy-start = (bf16[256,1024]{1,0:T(8,128)(2,1)S(1)}, bf16[256,1024]{1,0:T(8,128)(2,1)}, u32[]{:S(2)}) copy-start(bf16[256,1024]{1,0:T(8,128)(2,1)} %param.14) | copy-start | bytes 1572868
  10.5 25.5 %all-to-all-start = ((bf16[32,2,8,256]{3,2,1,0:T(8,128)(2,1)}), bf16[32,2,8,256]{3,2,1,0:T(8,128)(2,1)S(1)}, u32[]{:S(2)}, u32[]{:S(2)}) async-start(bf16[32,2,8,256]{3,2,1,0:T(8,128)(2,1)} %select_select_fusion.2), calls=%async_computation | async-start | bytes 524288 | tf_op jit(solution)/shard_map/all_to_all | solution.py:140
  23.1 102.6 %all-gather.2.cloned.1.call-start = ((), (), s32[]{:S(2)}) async-start(), calls=%async_computation.4 | async-start | bytes 4325376 | tf_op jit(solution)/shard_map/all_gather | solution.py:105
  38.3 5.6 %copy-start.3 = (s32[17]{0:T(128)S(1)}, s32[17]{0:T(128)}, u32[]{:S(2)}) copy-start(s32[17]{0:T(128)} %param.17) | copy-start | bytes 208
  38.3 6.7 %copy-start.2 = (s32[1024]{0:T(1024)S(1)}, s32[1024]{0:T(1024)}, u32[]{:S(2)}) copy-start(s32[1024]{0:T(1024)} %param.20) | copy-start | bytes 12292
  39.6 36.6 %all-to-all-start.1 = ((bf16[32,2,8,1024]{3,2,1,0:T(8,128)(2,1)}), bf16[32,2,8,1024]{3,2,1,0:T(8,128)(2,1)S(1)}, u32[]{:S(2)}, u32[]{:S(2)}) async-start(bf16[32,2,8,1024]{3,2,1,0:T(8,128)(2,1)} %bitcast.7), calls=%async_computation.1 | async-start | bytes 2097152 | tf_op jit(solution)/shard_map/all_to_all | solution.py:139
  76.2 49.5 %copy-start.1 = (s32[1024]{0:T(1024)S(1)}, s32[1024]{0:T(1024)}, u32[]{:S(2)}) copy-start(s32[1024]{0:T(1024)} %param.19) | copy-start | bytes 12292
  349.7 32.8 %all-to-all-start.2 = ((bf16[32,2,8,1024]{3,2,1,0:T(8,128)(2,1)}), bf16[32,2,8,1024]{3,2,1,0:T(8,128)(2,1)S(1)}, u32[]{:S(2)}, u32[]{:S(2)}) async-start(bf16[32,2,8,1024]{3,2,1,0:T(8,128)(2,1)} %bitcast.10), calls=%async_computation.2 | async-start | bytes 2097152 | tf_op jit(solution)/shard_map/all_to_all | solution.py:160
  354.4 88.3 %reduce-scatter.2.cloned.1.call-start = ((), (), s32[]{:S(2)}) async-start(), calls=%async_computation.5 | async-start | bytes 2359296 | tf_op jit(solution)/shard_map/reduce_scatter | solution.py:48
Sparse Core Ops, SparseCore 0:
  37.6 88.1 all-gather.1
  390.3 52.2 reduce-scatter.1
where the time goes:
time: 452 us; the launch traced here: 449 us
  waiting for transfers between devices  172 us (38%)
  matrix products  143 us (32%)
  local copies, waits for them, and re-layouts  57.4 us (13%)
  other arithmetic  38.7 us (9%)
  starting transfers between devices  21.4 us (5%)
  between operations  13.7 us (3%)
    dot_general x32, matrix products, one_step(): jnp.einsum('tkgs,skd->tkgd', weights.astype(jnp.bfloat16), value_heads, p...  93.9 us
    reduce_scatter x1, waiting for transfers between devices, project(): lax.psum_scatter(partial_value, 'head', scatter_dimension=1, tiled=True)  52.4 us
    all_gather x1, waiting for transfers between devices, attend_all(): kv_piece = lax.all_gather(held_pairs, 'ctx', axis=0, tiled=True)  48.6 us
    gather x32, local copies, waits for them, and re-layouts, key_position(): return jnp.take(inverse, key_ids // BLK) * BLK + key_ids % BLK  43.7 us
    dot_general x32, matrix products, one_step(): jnp.einsum('tkgd,skd->tkgs', query_heads, key_heads, preferred_element_ty...  42.1 us
    all_to_all x1, waiting for transfers between devices, on_device(): lax.all_to_all(send_queries, 'ctx', split_axis=0, concat_axis=0, tiled=True)  31 us
    all_to_all x1, waiting for transfers between devices, on_device(): lax.all_to_all(send_att, 'ctx', split_axis=0, concat_axis=0, tiled=True)  28.1 us
    reduce_sum x32, other arithmetic, one_step(): new_sum = run_sum * fading + jnp.sum(weights, axis=-1)  16.4 us
  transfers between devices with their start and end apart: 5, of which 5 were waited for; matrix products, arithmetic and copies ran while one was open for 1% of the time, Pallas kernels for 0%

commit v1 on v0

--- a/solution.py
+++ b/solution.py
@@ -102,7 +102,9 @@
         jnp.zeros(stat_shape, jnp.float32),
         jnp.zeros(stat_shape + (HD,), jnp.float32),
     )
-    kv_piece = lax.all_gather(held_pairs, "ctx", axis=0, tiled=True)
+    kv_piece = jnp.concatenate(
+        lax.all_to_all(jnp.stack([held_pairs] * lax.axis_size("ctx")), "ctx", 0, 0), axis=0
+    )
     piece_rows = kv_piece.shape[0]
     key_width = 256
 

time: 452 us -> 503 us (1.11)
  waiting for transfers between devices: 172 us -> 210 us
  starting transfers between devices: 21.4 us -> 30.2 us
    all_to_all x0 -> x1, waiting for transfers between devices: none -> 91.7 us  [attend_all(): lax.all_to_all(jnp.stack([held_pairs] * lax.axis_size('ctx')), 'ctx', 0, 0)]
    all_gather x1 -> x0, waiting for transfers between devices: 48.6 us -> none  [attend_all(): kv_piece = lax.all_gather(held_pairs, 'ctx', axis=0, tiled=True)]
    all_to_all x0 -> x1, starting transfers between devices: none -> 5.97 us  [attend_all(): lax.all_to_all(jnp.stack([held_pairs] * lax.axis_size('ctx')), 'ctx', 0, 0)]
where the time goes in v1:
time: 503 us; the launch traced here: 500 us
  waiting for transfers between devices  210 us (42%)
  matrix products  146 us (29%)
  local copies, waits for them, and re-layouts  59.9 us (12%)
  other arithmetic  37.3 us (7%)
  starting transfers between devices  30.2 us (6%)
  between operations  13.7 us (3%)
    dot_general x32, matrix products, one_step(): jnp.einsum('tkgs,skd->tkgd', weights.astype(jnp.bfloat16), value_heads, p...  96.7 us
    all_to_all x1, waiting for transfers between devices, attend_all(): lax.all_to_all(jnp.stack([held_pairs] * lax.axis_size('ctx')), 'ctx', 0, 0)  91.7 us
    reduce_scatter x1, waiting for transfers between devices, project(): lax.psum_scatter(partial_value, 'head', scatter_dimension=1, tiled=True)  52 us
    gather x32, local copies, waits for them, and re-layouts, key_position(): return jnp.take(inverse, key_ids // BLK) * BLK + key_ids % BLK  43.7 us
    dot_general x32, matrix products, one_step(): jnp.einsum('tkgd,skd->tkgs', query_heads, key_heads, preferred_element_ty...  42 us
    all_to_all x1, waiting for transfers between devices, on_device(): lax.all_to_all(send_att, 'ctx', split_axis=0, concat_axis=0, tiled=True)  28.1 us
    all_to_all x1, waiting for transfers between devices, on_device(): lax.all_to_all(send_queries, 'ctx', split_axis=0, concat_axis=0, tiled=True)  27 us
    reduce_sum x32, other arithmetic, one_step(): new_sum = run_sum * fading + jnp.sum(weights, axis=-1)  16.4 us
  transfers between devices with their start and end apart: 5, of which 5 were waited for; matrix products, arithmetic and copies ran while one was open for 1% of the time, Pallas kernels for 0%

profile of v1, /device:TPU:1, one launch (start us, length us, event | category | flops | bytes accessed | tf_op | source)
XLA Modules:
  0.0 499.7 jit_solution(6811969171896985589)
XLA Ops:
  10.5 12.6 %all-to-all-start = ((bf16[32,2,8,256]{3,2,1,0:T(8,128)(2,1)}), bf16[32,2,8,256]{3,2,1,0:T(8,128)(2,1)S(1)}, u32[]{:S(2)}, u32[]{:S(2)}) async-start(bf16[32,2,8,256]{3,2,1,0:T(8,128)(2,1)} %select_select_fusion.2), calls=%async_computation | async-start | bytes 524288 | tf_op jit(solution)/shard_map/all_to_all | solution.py:142
  25.2 10.8 %all-to-all-done = bf16[32,2,8,256]{3,2,1,0:T(8,128)(2,1)S(1)} async-done(((bf16[32,2,8,256]{3,2,1,0:T(8,128)(2,1)}), bf16[32,2,8,256]{3,2,1,0:T(8,128)(2,1)S(1)}, u32[]{:S(2)}, u32[]{:S(2)}) %all-to-all-start) | async-done | bytes 262176 | tf_op jit(solution)/shard_map/all_to_all | solution.py:142
  36.1 4.1 all-to-all-start.2
  41.4 27.0 %all-to-all-done.2 = bf16[32,2,8,1024]{3,2,1,0:T(8,128)(2,1)S(1)} async-done(((bf16[32,2,8,1024]{3,2,1,0:T(8,128)(2,1)}), bf16[32,2,8,1024]{3,2,1,0:T(8,128)(2,1)S(1)}, u32[]{:S(2)}, u32[]{:S(2)}) %all-to-all-start.2) | async-done | bytes 1048608 | tf_op jit(solution)/shard_map/all_to_all | solution.py:141
  68.4 2.4 stack.3
  70.8 6.0 %all-to-all-start.1 = ((bf16[32,256,256]{2,1,0:T(8,128)(2,1)}), bf16[32,256,256]{2,1,0:T(8,128)(2,1)}, u32[]{:S(2)}, u32[]{:S(2)}) async-start(bf16[32,256,256]{2,1,0:T(8,128)(2,1)} %stack.3), calls=%async_computation.1 | async-start | bytes 8388608 | tf_op jit(solution)/shard_map/all_to_all | solution.py:106
  79.2 91.7 %all-to-all-done.1 = bf16[32,256,256]{2,1,0:T(8,128)(2,1)} async-done(((bf16[32,256,256]{2,1,0:T(8,128)(2,1)}), bf16[32,256,256]{2,1,0:T(8,128)(2,1)}, u32[]{:S(2)}, u32[]{:S(2)}) %all-to-all-start.1) | async-done | bytes 4194336 | tf_op jit(solution)/shard_map/all_to_all | solution.py:106
  170.8 223.0 %while.21 = (s32[]{:T(128)}, f32[256,1,8]{0,2,1:T(8,128)S(1)}, f32[256,1,8]{0,2,1:T(8,128)S(1)}, f32[256,1,8,128]{0,3,2,1:T(8,128)}, s32[256]{0:T(256)S(1)}, /*i...) while((s32[]{:T(128)}, f32[256,1,8]{0,2,1:T(8,128)S(1)}, ...), condition=%wide.region_12.15_spmd.clone, body=%wide.region_8.14_spmd.clone.sunk | while | flops 276407808 | bytes 9464371 | solution.py:116
  174.2 2.6 fusion.44
  180.8 3.0 fusion.44
  184.4 1.4 gather_fusion
  187.8 3.0 fusion.44
  194.8 3.0 fusion.44
  201.7 3.0 fusion.44
  208.7 3.0 fusion.44
  215.7 3.0 fusion.44
  222.7 3.0 fusion.44
  229.7 3.0 fusion.44
  236.6 3.0 fusion.44
  240.3 1.4 gather_fusion
  243.6 3.0 fusion.44
  250.6 3.0 fusion.44
  257.6 3.0 fusion.44
  264.6 3.0 fusion.44
  271.5 3.0 fusion.44
  278.5 3.0 fusion.44
  285.5 3.0 fusion.44
  292.5 3.0 fusion.44
  296.1 1.4 gather_fusion
  299.5 3.0 fusion.44
  306.4 3.0 fusion.44
  313.4 3.0 fusion.44
  317.1 1.4 gather_fusion
  320.4 3.0 fusion.44
  327.4 3.0 fusion.44
  334.4 3.0 fusion.44
  341.4 3.0 fusion.44
  348.3 3.0 fusion.44
  355.3 3.0 fusion.44
  362.3 3.0 fusion.44
  369.3 3.0 fusion.44
  376.3 3.0 fusion.44
  383.2 3.0 fusion.44
  390.2 3.0 fusion.44
  397.5 7.5 %all-to-all-start.3 = ((bf16[32,2,8,1024]{3,2,1,0:T(8,128)(2,1)}), bf16[32,2,8,1024]{3,2,1,0:T(8,128)(2,1)S(1)}, u32[]{:S(2)}, u32[]{:S(2)}) async-start(bf16[32,2,8,1024]{3,2,1,0:T(8,128)(2,1)} %bitcast.11), calls=%async_computation.3 | async-start | bytes 2097152 | tf_op jit(solution)/shard_map/all_to_all | solution.py:162
  405.1 28.1 %all-to-all-done.3 = bf16[32,2,8,1024]{3,2,1,0:T(8,128)(2,1)S(1)} async-done(((bf16[32,2,8,1024]{3,2,1,0:T(8,128)(2,1)}), bf16[32,2,8,1024]{3,2,1,0:T(8,128)(2,1)S(1)}, u32[]{:S(2)}, u32[]{:S(2)}) %all-to-all-start.3) | async-done | bytes 1048608 | tf_op jit(solution)/shard_map/all_to_all | solution.py:162
  433.7 7.1 %convolution_convert_fusion = bf16[256,4096]{1,0:T(8,128)(2,1)} fusion(bf16[1024,4096]{1,0:T(8,128)(2,1)} %param.21, bf16[32,8,1024]{2,1,0:T(8,128)(2,1)S(1)} %gather_fusion.6, pred[32]{0:T(512)(128)(4,1)S(1)} %get-tuple-element.401), kind=kOutput, calls=%fused_computation.58 | convolution fusion | flops 2148794368 | bytes 11010080 | tf_op jit(solution)/shard_map/dot_general | solution.py:45
  440.9 52.0 %reduce-scatter.2.cloned.1.call-done = bf16[256,512]{1,0:T(8,128)(2,1)} async-done(((bf16[256,4096]{1,0:T(8,128)(2,1)}), bf16[256,512]{1,0:T(8,128)(2,1)}) %reduce-scatter.2.cloned.1.call-update) | async-done | bytes 262160 | tf_op jit(solution)/shard_map/reduce_scatter | solution.py:48
  (551 shorter events, 131.4 us)
Async XLA Ops:
  6.5 16.8 %copy-start = (bf16[256,1024]{1,0:T(8,128)(2,1)S(1)}, bf16[256,1024]{1,0:T(8,128)(2,1)}, u32[]{:S(2)}) copy-start(bf16[256,1024]{1,0:T(8,128)(2,1)} %param.14) | copy-start | bytes 1572868
  10.5 25.5 %all-to-all-start = ((bf16[32,2,8,256]{3,2,1,0:T(8,128)(2,1)}), bf16[32,2,8,256]{3,2,1,0:T(8,128)(2,1)S(1)}, u32[]{:S(2)}, u32[]{:S(2)}) async-start(bf16[32,2,8,256]{3,2,1,0:T(8,128)(2,1)} %select_select_fusion.2), calls=%async_computation | async-start | bytes 524288 | tf_op jit(solution)/shard_map/all_to_all | solution.py:142
  24.0 16.2 %copy-start.1 = (s32[1024]{0:T(1024)S(1)}, s32[1024]{0:T(1024)}, u32[]{:S(2)}) copy-start(s32[1024]{0:T(1024)} %param.19) | copy-start | bytes 12292
  36.1 32.3 %all-to-all-start.2 = ((bf16[32,2,8,1024]{3,2,1,0:T(8,128)(2,1)}), bf16[32,2,8,1024]{3,2,1,0:T(8,128)(2,1)S(1)}, u32[]{:S(2)}, u32[]{:S(2)}) async-start(bf16[32,2,8,1024]{3,2,1,0:T(8,128)(2,1)} %bitcast.8), calls=%async_computation.2 | async-start | bytes 2097152 | tf_op jit(solution)/shard_map/all_to_all | solution.py:141
  70.8 6.2 %copy-start.3 = (s32[17]{0:T(128)S(1)}, s32[17]{0:T(128)}, u32[]{:S(2)}) copy-start(s32[17]{0:T(128)} %param.17) | copy-start | bytes 208
  70.8 7.3 %copy-start.2 = (s32[1024]{0:T(1024)S(1)}, s32[1024]{0:T(1024)}, u32[]{:S(2)}) copy-start(s32[1024]{0:T(1024)} %param.20) | copy-start | bytes 12292
  70.8 100.0 %all-to-all-start.1 = ((bf16[32,256,256]{2,1,0:T(8,128)(2,1)}), bf16[32,256,256]{2,1,0:T(8,128)(2,1)}, u32[]{:S(2)}, u32[]{:S(2)}) async-start(bf16[32,256,256]{2,1,0:T(8,128)(2,1)} %stack.3), calls=%async_computation.1 | async-start | bytes 8388608 | tf_op jit(solution)/shard_map/all_to_all | solution.py:106
  397.5 35.6 %all-to-all-start.3 = ((bf16[32,2,8,1024]{3,2,1,0:T(8,128)(2,1)}), bf16[32,2,8,1024]{3,2,1,0:T(8,128)(2,1)S(1)}, u32[]{:S(2)}, u32[]{:S(2)}) async-start(bf16[32,2,8,1024]{3,2,1,0:T(8,128)(2,1)} %bitcast.11), calls=%async_computation.3 | async-start | bytes 2097152 | tf_op jit(solution)/shard_map/all_to_all | solution.py:162
  405.0 87.9 %reduce-scatter.2.cloned.1.call-start = ((), (), s32[]{:S(2)}) async-start(), calls=%async_computation.5 | async-start | bytes 2359296 | tf_op jit(solution)/shard_map/reduce_scatter | solution.py:48
Sparse Core Ops, SparseCore 0:
  441.0 51.8 reduce-scatter.1
